TPU v7x, 32 devices: a whole 2x2x4 slice. The times are simulated.
32 devices in a mesh: box: 4 (over z), row: 4 (over y, core), col: 2 (over x).
Axes of the slice: x: 2, y: 2, z: 4, core: 2. Of those that a mesh axis runs over, the one named last changes fastest.
Arguments:
- ext_ext: float32 [4, 3072, 3072], P('box', 'row', 'col'), may hold values from -6 to 6
- ext_int: float32 [4, 3072, 1024], P('box', 'row', 'col'), may hold values from -0.1875 to 0.1875
- int_ext: float32 [4, 1024, 3072], P('box', 'row', 'col'), may hold values from -6 to 6
- int_int: float32 [4, 1024, 1024], P('box', 'row', 'col'), may hold values from -0.1 to 0.1, as said below
Outputs:
- merged: float32 [4, 3072, 2, 3072], P('box', 'row', None, 'col')
Inputs may be any that keep to these rules, and one draw needn't show every extreme that they name: `int_int`: independent entries.
All inputs are finite; a program needn't handle non-finite values.
Results may differ from a plain program's by a relative error of at most 0.0003.
Values sent between devices are 32-bit elements; how exact they have to be, the bound alone decides.
No kernel may reach another device: no remote copies, remote signals or barrier semaphores. Data moves between devices by JAX's collectives and lax.ppermute only.
A program may use at most 128 MiB of HBM per device.

v0:
```python
import jax
import jax.numpy as jnp
from jax import lax
from jax.sharding import PartitionSpec as P

HIGH = lax.Precision.HIGHEST


def swapped(shard, axis, distance):
    return lax.ppermute(shard, axis, [(i, i ^ 1 << distance) for i in range(lax.axis_size(axis))])


def panel_dot(total, piece, panel):
    return total + jnp.dot(piece, panel, precision=HIGH, preferred_element_type=jnp.float32)


def chain_product(left, right):
    panel = lax.all_gather(right, "row", axis=0, tiled=True)
    empty = jnp.zeros((left.shape[0], right.shape[1]), jnp.float32)
    return panel_dot(empty, lax.all_gather(left, "col", axis=1, tiled=True), panel)


def local(ext_ext, ext_int, int_ext, int_int):
    own_ee = ext_ext[0]
    own_ed = ext_int[0]
    own_de = int_ext[0]
    own_dd = int_int[0]
    partner_dd, partner_de = swapped((own_dd, own_de), "box", 0)
    is_even = lax.axis_index("box") % 2 == 0
    block_rows = own_dd.shape[0]
    block_cols = own_dd.shape[1]
    row_ids = lax.axis_index("row") * block_rows + lax.broadcasted_iota(
        jnp.int32, (block_rows, block_cols), 0
    )
    col_ids = lax.axis_index("col") * block_cols + lax.broadcasted_iota(
        jnp.int32, (block_rows, block_cols), 1
    )
    identity = (row_ids == col_ids).astype(jnp.float32)
    coupling = chain_product(partner_dd, own_dd)
    square = chain_product(coupling, coupling)
    first = identity + coupling
    inverse = first + chain_product(first, square)
    de_panel = lax.all_gather(own_de, "row", axis=0, tiled=True)
    coupled = panel_dot(
        jnp.zeros(own_de.shape, jnp.float32),
        lax.all_gather(partner_dd, "col", axis=1, tiled=True),
        de_panel,
    )
    source = jnp.concatenate(
        [jnp.where(is_even, coupled, partner_de), jnp.where(is_even, partner_de, coupled)], axis=1
    )
    source_panel = lax.all_gather(source, "row", axis=0, tiled=True)
    pieces = lax.all_gather(inverse[None], ("row", "col"), axis=0, tiled=True)
    row_count = lax.axis_size("row")
    col_count = lax.axis_size("col")
    whole = pieces.reshape(row_count, col_count, block_rows, block_cols).transpose(0, 2, 1, 3)
    whole = whole.reshape(row_count * block_rows, col_count * block_cols)
    right_panel = jnp.dot(whole, source_panel, precision=HIGH, preferred_element_type=jnp.float32)
    zeros = jnp.zeros_like(own_ee)
    start_terms = jnp.concatenate(
        [jnp.where(is_even, own_ee, zeros), jnp.where(is_even, zeros, own_ee)], axis=1
    )
    merged = panel_dot(start_terms, lax.all_gather(own_ed, "col", axis=1, tiled=True), right_panel)
    return merged.reshape(1, own_ee.shape[0], 2, own_ee.shape[1])


def solution(mesh):
    placed = (
        P("box", "row", "col"),
        P("box", "row", "col"),
        P("box", "row", "col"),
        P("box", "row", "col"),
    )
    return jax.shard_map(
        local, mesh=mesh, in_specs=placed, out_specs=P("box", "row", None, "col"), check_vma=False
    )
```

profile of v0, /device:TPU:0, one launch (start us, length us, event | category | flops | bytes accessed | tf_op | source)
XLA Modules:
  0.0 469.0 jit_solution(2206762846612566274)
XLA Ops:
  6.5 0.0 all-gather.15.cloned.1.call-start
  6.5 3.1 collective-permute-start
  9.6 12.1 %collective-permute-done = f32[256,512]{1,0:T(8,128)S(1)} collective-permute-done((f32[256,512]{1,0:T(8,128)}, f32[256,512]{1,0:T(8,128)S(1)}, u32[]{:S(2)}, u32[]{:S(2)}) %collective-permute-start) | collective-permute-done | bytes 524320 | tf_op jit(solution)/shard_map/ppermute | solution.py:10
  21.7 0.8 copy-done.2
  22.5 0.0 all-gather.15.cloned.1.call-update
  22.5 0.0 all-gather.27.cloned.1.call-start
  22.6 0.7 all-gather.27.cloned.1.call-update
  23.3 0.0 all-gather.19.cloned.1.call-start
  23.4 22.0 %all-gather.15.cloned.1.call-done = f32[256,1024]{1,0:T(8,128)} async-done(((f32[256,512]{1,0:T(8,128)}), f32[256,1024]{1,0:T(8,128)}) %all-gather.15.cloned.1.call-update) | async-done | bytes 1048592 | tf_op jit(solution)/shard_map/all_gather | solution.py:20
  45.4 24.2 %all-gather.27.cloned.1.call-done = f32[1,1024,512]{2,1,0:T(8,128)} async-done(((f32[1,256,512]{2,1,0:T(8,128)}), f32[1,1024,512]{2,1,0:T(8,128)}) %all-gather.27.cloned.1.call-update) | async-done | bytes 2097168 | tf_op jit(solution)/shard_map/all_gather | solution.py:18
  69.5 4.8 %convert_add_fusion = (f32[256,512]{1,0:T(8,128)}, f32[256,512]{1,0:T(8,128)}) fusion(s32[512]{0:T(512)S(1)} %iota_add_fusion, s32[256]{0:T(256)S(1)} %iota_add_fusion.1, f32[256,1024]{1,0:T(8,128)} %all-gather.15.cloned.1.call-done, f32[1,1024,512]{2,1,0:T(8,128)} %all-gather.27.cloned.1.call-done), kind=kOutput, calls=%fused_computation.12 | convolution fusion | flops 1611005952 | bytes 4197376 | tf_op jit(solution)/shard_map/dot_general | solution.py:14
  74.4 0.0 all-gather.19.cloned.1.call-update
  74.4 0.0 all-gather.21.cloned.1.call-start
  74.4 0.5 all-gather.21.cloned.1.call-update
  75.0 0.0 all-gather.17.cloned.1.call-start
  75.0 0.5 all-gather.17.cloned.1.call-update
  75.6 0.0 all-gather.23.cloned.1.call-start
  75.6 20.2 %all-gather.19.cloned.1.call-done = f32[256,1024]{1,0:T(8,128)} async-done(((f32[256,512]{1,0:T(8,128)}), f32[256,1024]{1,0:T(8,128)}) %all-gather.19.cloned.1.call-update) | async-done | bytes 1048592 | tf_op jit(solution)/shard_map/all_gather | solution.py:20
  95.8 24.0 %all-gather.21.cloned.1.call-done = f32[1024,512]{1,0:T(8,128)} async-done(((f32[256,512]{1,0:T(8,128)}), f32[1024,512]{1,0:T(8,128)}) %all-gather.21.cloned.1.call-update) | async-done | bytes 2097168 | tf_op jit(solution)/shard_map/all_gather | solution.py:18
  119.8 4.6 fusion.5
  124.5 0.0 all-gather.23.cloned.1.call-update
  124.5 0.0 all-gather.31.cloned.1.call-start
  124.6 0.7 all-gather.31.cloned.1.call-update
  125.3 0.0 all-gather.29.cloned.1.call-start
  125.3 17.2 %all-gather.17.cloned.1.call-done = f32[256,1024]{1,0:T(8,128)} async-done(((f32[256,512]{1,0:T(8,128)}), f32[256,1024]{1,0:T(8,128)}) %all-gather.17.cloned.1.call-update) | async-done | bytes 1048592 | tf_op jit(solution)/shard_map/all_gather | solution.py:20
  142.5 24.0 %all-gather.23.cloned.1.call-done = f32[1024,512]{1,0:T(8,128)} async-done(((f32[256,512]{1,0:T(8,128)}), f32[1024,512]{1,0:T(8,128)}) %all-gather.23.cloned.1.call-update) | async-done | bytes 2097168 | tf_op jit(solution)/shard_map/all_gather | solution.py:18
  166.6 0.0 copy-done
  166.6 4.6 convolution_add_fusion
  171.2 0.0 all-gather.29.cloned.1.call-update
  171.2 0.0 all-gather.25.cloned.1.call-start
  171.3 1.6 collective-permute-start.1
  172.8 35.3 %collective-permute-done.1 = f32[256,1536]{1,0:T(8,128)S(1)} collective-permute-done((f32[256,1536]{1,0:T(8,128)}, f32[256,1536]{1,0:T(8,128)S(1)}, u32[]{:S(2)}, u32[]{:S(2)}) %collective-permute-start.1) | collective-permute-done | bytes 1572896 | tf_op jit(solution)/shard_map/ppermute | solution.py:10
  208.1 6.4 %all-gather.31.cloned.1.call-done = f32[1,1024,1536]{2,1,0:T(8,128)} async-done(((f32[1,256,1536]{2,1,0:T(8,128)}), f32[1,1024,1536]{2,1,0:T(8,128)}) %all-gather.31.cloned.1.call-update) | async-done | bytes 6291472 | tf_op jit(solution)/shard_map/all_gather | solution.py:43
  214.5 7.6 %broadcast_select_fusion.1 = (f32[256,1536]{1,0:T(8,128)S(1)}, f32[256,1536]{1,0:T(8,128)S(1)}) fusion(f32[256,1536]{1,0:T(8,128)S(1)} %collective-permute-done.1, pred[]{:T(512)S(6)} %eq.8, f32[256,1024]{1,0:T(8,128)S(1)} %copy-done.1, f32[1,1024,1536]{2,1,0:T(8,128)} %all-gather.31.cloned.1.call-done), kind=kOutput, calls=%fused_computation.11 | convolution fusion | flops 4832624640 | bytes 12058625 | tf_op jit(solution)/shard_map/dot_general | solution.py:14
  222.1 1.9 pad_maximum_fusion
  224.1 0.0 all-gather.25.cloned.1.call-update
  224.1 0.2 all-gather.33.cloned.1.call-start
  224.3 0.4 all-gather.33.cloned.1.call-update
  224.7 6.1 %copy.8 = f32[1,768,1536]{1,2,0:T(8,128)} copy(f32[1,768,1536]{2,1,0:T(8,128)} %param.4) | data formatting | bytes 9437184 | tf_op args[0]
  230.7 6.7 %select_bitcast_fusion.1 = (f32[768,1536]{0,1:T(8,128)}, f32[768,1536]{0,1:T(8,128)}) fusion(f32[1,768,1536]{1,2,0:T(8,128)} %copy.8, pred[]{:T(512)S(6)} %eq.8), kind=kLoop, calls=%fused_computation.4 | loop fusion | flops 2359296 | bytes 14155777 | tf_op jit(solution)/shard_map/jit(_where)/select_n | solution.py:61
  237.4 15.6 %all-gather.29.cloned.1.call-done = f32[2048,512]{1,0:T(8,128)} async-done(((f32[256,512]{1,0:T(8,128)}), f32[2048,512]{1,0:T(8,128)}) %all-gather.29.cloned.1.call-update) | async-done | bytes 4194320 | tf_op jit(solution)/shard_map/all_gather | solution.py:53
  253.0 5.4 %copy.10 = f32[4,2,256,512]{3,1,2,0:T(2,128)S(1)} copy(f32[4,2,256,512]{3,2,1,0:T(8,128)} %bitcast.38) | data formatting | bytes 8388608 | tf_op jit(solution)/shard_map/reshape | solution.py:56
  258.4 3.1 copy.12
  261.5 75.2 %all-gather.25.cloned.1.call-done = f32[1024,3072]{1,0:T(8,128)} async-done(((f32[256,3072]{1,0:T(8,128)}), f32[1024,3072]{1,0:T(8,128)}) %all-gather.25.cloned.1.call-update) | async-done | bytes 12582928 | tf_op jit(solution)/shard_map/all_gather | solution.py:52
  336.7 44.8 %fusion.6 = f32[1024,3072]{1,0:T(8,128)} fusion(f32[1024,1024]{1,0:T(8,128)} %bitcast.39, f32[1024,3072]{1,0:T(8,128)} %all-gather.25.cloned.1.call-done), kind=kOutput, calls=%fused_computation.16 | convolution fusion | flops 38654705664 | bytes 29360128 | tf_op jit(solution)/shard_map/dot_general | solution.py:58
  381.4 1.6 all-gather.33.cloned.1.call-done
  383.0 64.4 %maximum_add_fusion = f32[768,3072]{0,1:T(8,128)} fusion(f32[768,1536]{0,1:T(8,128)} %get-tuple-element.6, f32[768,1536]{0,1:T(8,128)} %get-tuple-element.5, f32[1024,3072]{1,0:T(8,128)} %fusion.6, f32[1,768,1024]{2,1,0:T(8,128)} %all-gather.33.cloned.1.call-done), kind=kOutput, calls=%fused_computation | convolution fusion | flops 28995747840 | bytes 34603008 | tf_op jit(solution)/shard_map/dot_general | solution.py:14
  447.4 14.8 %copy.11 = f32[1,768,2,1536]{3,2,1,0:T(2,128)} copy(f32[1,768,2,1536]{1,3,2,0:T(8,128)} %bitcast.37) | data formatting | bytes 18874368 | tf_op jit(solution)/shard_map/reshape | solution.py:64
  (6 shorter events, 0.0 us)
Async XLA Ops:
  6.5 38.9 %all-gather.15.cloned.1.call-start = ((), (), s32[]{:S(2)}) async-start(), calls=%async_computation | async-start | bytes 1572864 | tf_op jit(solution)/shard_map/all_gather | solution.py:20
  6.5 15.2 %collective-permute-start = (f32[256,512]{1,0:T(8,128)}, f32[256,512]{1,0:T(8,128)S(1)}, u32[]{:S(2)}, u32[]{:S(2)}) collective-permute-start(f32[256,512]{1,0:T(8,128)} %bitcast.41), channel_id=1, source_target_pairs={{0,8},{8,0},{16,24},{24,16},{1,9},{9,1},{17,25},{25,17},{2,10},{10... | collective-permute-start | bytes 1572872 | tf_op jit(solution)/shard_map/ppermute | solution.py:10
  21.7 0.8 copy-start.2
  22.5 47.0 %all-gather.27.cloned.1.call-start = ((), (), s32[]{:S(2)}) async-start(), calls=%async_computation.6 | async-start | bytes 2621440 | tf_op jit(solution)/shard_map/all_gather | solution.py:18
  23.3 72.5 %all-gather.19.cloned.1.call-start = ((), (), s32[]{:S(2)}) async-start(), calls=%async_computation.2 | async-start | bytes 1572864 | tf_op jit(solution)/shard_map/all_gather | solution.py:20
  74.4 92.2 %copy-start = (f32[256,512]{1,0:T(8,128)S(1)}, f32[256,512]{1,0:T(8,128)}, u32[]{:S(2)}) copy-start(f32[256,512]{1,0:T(8,128)} %get-tuple-element.9) | copy-start | bytes 1572868
  74.4 45.4 %all-gather.21.cloned.1.call-start = ((), (), s32[]{:S(2)}) async-start(), calls=%async_computation.3 | async-start | bytes 2621440 | tf_op jit(solution)/shard_map/all_gather | solution.py:18
  75.0 67.6 %all-gather.17.cloned.1.call-start = ((), (), s32[]{:S(2)}) async-start(), calls=%async_computation.1 | async-start | bytes 1572864 | tf_op jit(solution)/shard_map/all_gather | solution.py:20
  75.6 91.0 %all-gather.23.cloned.1.call-start = ((), (), s32[]{:S(2)}) async-start(), calls=%async_computation.4 | async-start | bytes 2621440 | tf_op jit(solution)/shard_map/all_gather | solution.py:18
  124.5 90.0 %copy-start.1 = (f32[256,1024]{1,0:T(8,128)S(1)}, f32[256,1024]{1,0:T(8,128)}, u32[]{:S(2)}) copy-start(f32[256,1024]{1,0:T(8,128)} %all-gather.15.cloned.1.call-done) | copy-start | bytes 3145732
  124.5 90.0 %all-gather.31.cloned.1.call-start = ((), (), s32[]{:S(2)}) async-start(), calls=%async_computation.8 | async-start | bytes 7864320 | tf_op jit(solution)/shard_map/all_gather | solution.py:43
  125.3 127.7 %all-gather.29.cloned.1.call-start = ((), (), s32[]{:S(2)}) async-start(), calls=%async_computation.7 | async-start | bytes 4718592 | tf_op jit(solution)/shard_map/all_gather | solution.py:53
  171.2 165.5 %all-gather.25.cloned.1.call-start = ((), (), s32[]{:S(2)}) async-start(), calls=%async_computation.5 | async-start | bytes 15728640 | tf_op jit(solution)/shard_map/all_gather | solution.py:52
  171.3 36.8 %collective-permute-start.1 = (f32[256,1536]{1,0:T(8,128)}, f32[256,1536]{1,0:T(8,128)S(1)}, u32[]{:S(2)}, u32[]{:S(2)}) collective-permute-start(f32[256,1536]{1,0:T(8,128)} %bitcast.40), channel_id=1, source_target_pairs={{0,8},{8,0},{16,24},{24,16},{1,9},{9,1},{17,25},{25,17},{2,10},{10... | collective-permute-start | bytes 4718600 | tf_op jit(solution)/shard_map/ppermute | solution.py:10
  224.1 158.9 %all-gather.33.cloned.1.call-start = ((), (), s32[]{:S(2)}) async-start(), calls=%async_computation.9 | async-start | bytes 4718592 | tf_op jit(solution)/shard_map/all_gather | solution.py:63
Sparse Core Ops, SparseCore 0:
  22.7 22.6 all-gather.14
  46.9 22.5 all-gather.26
  74.5 21.2 all-gather.18
  97.2 22.5 all-gather.20
  121.2 21.2 all-gather.16
  143.9 22.5 all-gather.22
  168.1 46.3 all-gather.30
  216.4 36.5 all-gather.28
  254.6 82.0 all-gather.24
  338.1 44.8 all-gather.32
where the time goes:
time: 470 us; the launch traced here: 469 us
  waiting for transfers between devices  281 us (60%)
  matrix products  131 us (28%)
  local copies, waits for them, and re-layouts  30.1 us (6%)
  between operations  13.6 us (3%)
  other arithmetic  8.65 us (2%)
  starting transfers between devices  5.14 us (1%)
    dot_general x5, matrix products, panel_dot(): jnp.dot(piece, panel, precision=HIGH, preferred_element_type=jnp.float32)  86.1 us
    all_gather x1, waiting for transfers between devices, local(): source_panel = lax.all_gather(source, 'row', axis=0, tiled=True)  75.2 us
    all_gather x3, waiting for transfers between devices, chain_product(): panel = lax.all_gather(right, 'row', axis=0, tiled=True)  72.2 us
    all_gather x3, waiting for transfers between devices, chain_product(): lax.all_gather(left, 'col', axis=1, tiled=True)  59.5 us
    ppermute x2, waiting for transfers between devices, swapped(): lax.ppermute(shard, axis, [(i, i ^ 1 << distance) for i in range(lax.axis...  47.4 us
    dot_general x1, matrix products, local(): jnp.dot(whole, source_panel, precision=HIGH, preferred_element_type=jnp.f...  44.8 us
    all_gather x1, waiting for transfers between devices, local(): pieces = lax.all_gather(inverse[None], ('row', 'col'), axis=0, tiled=True)  15.6 us
    reshape x1, local copies, waits for them, and re-layouts, local(): return merged.reshape(1, own_ee.shape[0], 2, own_ee.shape[1])  14.8 us
  transfers between devices with their start and end apart: 12, of which 12 were waited for; matrix products, arithmetic and copies ran while one was open for 18% of the time, Pallas kernels for 0%

commit v1 on v0

--- a/solution.py
+++ b/solution.py
@@ -17,7 +17,7 @@
 def chain_product(left, right):
     panel = lax.all_gather(right, "row", axis=0, tiled=True)
     empty = jnp.zeros((left.shape[0], right.shape[1]), jnp.float32)
-    return panel_dot(empty, lax.all_gather(left, "col", axis=1, tiled=True), panel)
+    return panel_dot(empty, jnp.concatenate(lax.all_gather(left, "col"), axis=1), panel)
 
 
 def local(ext_ext, ext_int, int_ext, int_int):

time: 470 us -> 492 us (1.047)
  waiting for transfers between devices: 281 us -> 299 us
    all_gather x1, waiting for transfers between devices: 6.43 us -> 29.8 us  [local(): de_panel = lax.all_gather(own_de, 'row', axis=0, tiled=True)]
    ppermute x2, waiting for transfers between devices: 47.4 us -> 30.3 us  [swapped(): lax.ppermute(shard, axis, [(i, i ^ 1 << distance) for i in range(lax.axis...]
    all_gather x3 -> x4, waiting for transfers between devices: 59.5 us -> 75.8 us  [the longest x3 59 us: chain_product(): lax.all_gather(left, 'col')]
  transfers between devices with their start and end apart: 12 -> 13, of which waited for: 12 -> 13; matrix products, arithmetic and copies ran while one was open for 18% -> 18% of each run, Pallas kernels for 0% -> 0%
where the time goes in v1:
time: 492 us; the launch traced here: 491 us
  waiting for transfers between devices  299 us (61%)
  matrix products  130 us (26%)
  local copies, waits for them, and re-layouts  34.8 us (7%)
  between operations  13.3 us (3%)
  other arithmetic  8.65 us (2%)
  starting transfers between devices  5.18 us (1%)
    dot_general x5, matrix products, panel_dot(): jnp.dot(piece, panel, precision=HIGH, preferred_element_type=jnp.float32)  85.5 us
    all_gather x1, waiting for transfers between devices, local(): source_panel = lax.all_gather(source, 'row', axis=0, tiled=True)  75 us
    all_gather x3, waiting for transfers between devices, chain_product(): panel = lax.all_gather(right, 'row', axis=0, tiled=True)  67.5 us
    all_gather x3, waiting for transfers between devices, chain_product(): lax.all_gather(left, 'col')  59 us
    dot_general x1, matrix products, local(): jnp.dot(whole, source_panel, precision=HIGH, preferred_element_type=jnp.f...  44.7 us
    ppermute x2, waiting for transfers between devices, swapped(): lax.ppermute(shard, axis, [(i, i ^ 1 << distance) for i in range(lax.axis...  30.3 us
    all_gather x1, waiting for transfers between devices, local(): de_panel = lax.all_gather(own_de, 'row', axis=0, tiled=True)  29.8 us
    all_gather x1, waiting for transfers between devices, local(): lax.all_gather(partner_dd, 'col', axis=1, tiled=True)  16.9 us
  transfers between devices with their start and end apart: 13, of which 13 were waited for; matrix products, arithmetic and copies ran while one was open for 18% of the time, Pallas kernels for 0%

profile of v1, /device:TPU:0, one launch (start us, length us, event | category | flops | bytes accessed | tf_op | source)
XLA Modules:
  0.0 491.2 jit_solution(2488420305270122120)
XLA Ops:
  6.5 3.1 collective-permute-start
  9.6 12.1 %collective-permute-done = f32[256,512]{1,0:T(8,128)S(1)} collective-permute-done((f32[256,512]{1,0:T(8,128)}, f32[256,512]{1,0:T(8,128)S(1)}, u32[]{:S(2)}, u32[]{:S(2)}) %collective-permute-start) | collective-permute-done | bytes 524320 | tf_op jit(solution)/shard_map/ppermute | solution.py:10
  21.7 0.8 copy-done.1
  22.5 0.0 all-gather.27.cloned.1.call-update
  22.5 0.0 all-gather.29.cloned.1.call-start
  22.6 0.7 all-gather.29.cloned.1.call-update
  23.3 0.0 all-gather.33.cloned.1.call-start
  23.4 22.0 %all-gather.27.cloned.1.call-done = f32[512,512]{1,0:T(8,128)} async-done(((f32[256,512]{1,0:T(8,128)}), f32[512,512]{1,0:T(8,128)}) %all-gather.27.cloned.1.call-update) | async-done | bytes 1048592 | tf_op jit(solution)/shard_map/all_gather | solution.py:20
  45.4 1.6 copy.16
  46.9 22.6 %all-gather.29.cloned.1.call-done = f32[1,1024,512]{2,1,0:T(8,128)} async-done(((f32[1,256,512]{2,1,0:T(8,128)}), f32[1,1024,512]{2,1,0:T(8,128)}) %all-gather.29.cloned.1.call-update) | async-done | bytes 2097168 | tf_op jit(solution)/shard_map/all_gather | solution.py:18
  69.5 4.5 convert_add_fusion
  74.1 0.0 all-gather.19.cloned.1.call-start
  74.1 0.5 all-gather.19.cloned.1.call-update
  74.7 0.0 all-gather.31.cloned.1.call-start
  74.7 0.5 all-gather.31.cloned.1.call-update
  75.2 0.0 all-gather.21.cloned.1.call-start
  75.3 20.2 %all-gather.33.cloned.1.call-done = f32[512,512]{1,0:T(8,128)} async-done(((f32[256,512]{1,0:T(8,128)}), f32[512,512]{1,0:T(8,128)}) %all-gather.33.cloned.1.call-update) | async-done | bytes 1048592 | tf_op jit(solution)/shard_map/all_gather | solution.py:20
  95.5 1.6 copy.18
  97.1 22.5 %all-gather.19.cloned.1.call-done = f32[1024,512]{1,0:T(8,128)} async-done(((f32[256,512]{1,0:T(8,128)}), f32[1024,512]{1,0:T(8,128)}) %all-gather.19.cloned.1.call-update) | async-done | bytes 2097168 | tf_op jit(solution)/shard_map/all_gather | solution.py:18
  119.5 4.4 fusion.5
  123.9 0.0 all-gather.23.cloned.1.call-start
  124.0 0.7 all-gather.23.cloned.1.call-update
  124.7 0.0 all-gather.37.cloned.1.call-start
  124.7 0.7 all-gather.37.cloned.1.call-update
  125.5 0.0 all-gather.35.cloned.1.call-start
  125.5 16.7 %all-gather.31.cloned.1.call-done = f32[512,512]{1,0:T(8,128)} async-done(((f32[256,512]{1,0:T(8,128)}), f32[512,512]{1,0:T(8,128)}) %all-gather.31.cloned.1.call-update) | async-done | bytes 1048592 | tf_op jit(solution)/shard_map/all_gather | solution.py:20
  142.2 1.6 copy.17
  143.8 22.5 %all-gather.21.cloned.1.call-done = f32[1024,512]{1,0:T(8,128)} async-done(((f32[256,512]{1,0:T(8,128)}), f32[1024,512]{1,0:T(8,128)}) %all-gather.21.cloned.1.call-update) | async-done | bytes 2097168 | tf_op jit(solution)/shard_map/all_gather | solution.py:18
  166.2 4.3 convolution_add_fusion
  170.6 0.0 all-gather.25.cloned.1.call-start
  170.7 1.5 collective-permute-start.1
  172.2 16.9 %all-gather.23.cloned.1.call-done = f32[256,1024]{1,0:T(8,128)} async-done(((f32[256,512]{1,0:T(8,128)}), f32[256,1024]{1,0:T(8,128)}) %all-gather.23.cloned.1.call-update) | async-done | bytes 1048592 | tf_op jit(solution)/shard_map/all_gather | solution.py:46
  189.1 18.2 %collective-permute-done.1 = f32[256,1536]{1,0:T(8,128)S(1)} collective-permute-done((f32[256,1536]{1,0:T(8,128)S(1)}, f32[256,1536]{1,0:T(8,128)S(1)}, u32[]{:S(2)}, u32[]{:S(2)}) %collective-permute-start.1) | collective-permute-done | bytes 1572896 | tf_op jit(solution)/shard_map/ppermute | solution.py:10
  207.2 29.8 %all-gather.37.cloned.1.call-done = f32[1,1024,1536]{2,1,0:T(8,128)} async-done(((f32[1,256,1536]{2,1,0:T(8,128)}), f32[1,1024,1536]{2,1,0:T(8,128)}) %all-gather.37.cloned.1.call-update) | async-done | bytes 6291472 | tf_op jit(solution)/shard_map/all_gather | solution.py:43
  237.0 7.9 %broadcast_select_fusion.1 = (f32[256,1536]{1,0:T(8,128)S(1)}, f32[256,1536]{1,0:T(8,128)S(1)}) fusion(f32[256,1536]{1,0:T(8,128)S(1)} %collective-permute-done.1, pred[]{:T(512)S(6)} %eq.8, f32[256,1024]{1,0:T(8,128)} %all-gather.23.cloned.1.call-done, f32[1,1024,1536]{2,1,0:T(8,128)} %all-gather.37.cloned.1.call-done), kind=kOutput, calls=%fused_computation.11 | convolution fusion | flops 4832624640 | bytes 12058625 | tf_op jit(solution)/shard_map/dot_general | solution.py:14
  245.0 1.9 pad_maximum_fusion
  246.9 0.2 all-gather.39.cloned.1.call-start
  247.1 0.5 all-gather.39.cloned.1.call-update
  247.6 6.0 %copy.14 = f32[1,768,1536]{1,2,0:T(8,128)} copy(f32[1,768,1536]{2,1,0:T(8,128)} %param.4) | data formatting | bytes 9437184 | tf_op args[0]
  253.7 6.7 %select_bitcast_fusion.1 = (f32[768,1536]{0,1:T(8,128)}, f32[768,1536]{0,1:T(8,128)}) fusion(f32[1,768,1536]{1,2,0:T(8,128)} %copy.14, pred[]{:T(512)S(6)} %eq.8), kind=kLoop, calls=%fused_computation.4 | loop fusion | flops 2359296 | bytes 14155777 | tf_op jit(solution)/shard_map/jit(_where)/select_n | solution.py:61
  260.4 15.1 %all-gather.35.cloned.1.call-done = f32[2048,512]{1,0:T(8,128)} async-done(((f32[256,512]{1,0:T(8,128)}), f32[2048,512]{1,0:T(8,128)}) %all-gather.35.cloned.1.call-update) | async-done | bytes 4194320 | tf_op jit(solution)/shard_map/all_gather | solution.py:53
  275.5 5.4 %copy.19 = f32[4,2,256,512]{3,1,2,0:T(2,128)S(1)} copy(f32[4,2,256,512]{3,2,1,0:T(8,128)} %bitcast.51) | data formatting | bytes 8388608 | tf_op jit(solution)/shard_map/reshape | solution.py:56
  281.0 3.1 copy.21
  284.1 75.0 %all-gather.25.cloned.1.call-done = f32[1024,3072]{1,0:T(8,128)} async-done(((f32[256,3072]{1,0:T(8,128)}), f32[1024,3072]{1,0:T(8,128)}) %all-gather.25.cloned.1.call-update) | async-done | bytes 12582928 | tf_op jit(solution)/shard_map/all_gather | solution.py:52
  359.1 44.7 %fusion.6 = f32[1024,3072]{1,0:T(8,128)} fusion(f32[1024,1024]{1,0:T(8,128)} %bitcast.52, f32[1024,3072]{1,0:T(8,128)} %all-gather.25.cloned.1.call-done), kind=kOutput, calls=%fused_computation.16 | convolution fusion | flops 38654705664 | bytes 29360128 | tf_op jit(solution)/shard_map/dot_general | solution.py:58
  403.8 1.7 all-gather.39.cloned.1.call-done
  405.5 64.4 %maximum_add_fusion = f32[768,3072]{0,1:T(8,128)} fusion(f32[768,1536]{0,1:T(8,128)} %get-tuple-element.6, f32[768,1536]{0,1:T(8,128)} %get-tuple-element.5, f32[1024,3072]{1,0:T(8,128)} %fusion.6, f32[1,768,1024]{2,1,0:T(8,128)} %all-gather.39.cloned.1.call-done), kind=kOutput, calls=%fused_computation | convolution fusion | flops 28995747840 | bytes 34603008 | tf_op jit(solution)/shard_map/dot_general | solution.py:14
  469.9 14.8 %copy.20 = f32[1,768,2,1536]{3,2,1,0:T(2,128)} copy(f32[1,768,2,1536]{1,3,2,0:T(8,128)} %bitcast.49) | data formatting | bytes 18874368 | tf_op jit(solution)/shard_map/reshape | solution.py:64
  (12 shorter events, 0.1 us)
Async XLA Ops:
  6.5 38.9 %all-gather.27.cloned.1.call-start = ((), (), s32[]{:S(2)}) async-start(), calls=%async_computation.4 | async-start | bytes 1572864 | tf_op jit(solution)/shard_map/all_gather | solution.py:20
  6.5 15.2 %collective-permute-start = (f32[256,512]{1,0:T(8,128)}, f32[256,512]{1,0:T(8,128)S(1)}, u32[]{:S(2)}, u32[]{:S(2)}) collective-permute-start(f32[256,512]{1,0:T(8,128)} %bitcast.59), channel_id=1, source_target_pairs={{0,8},{8,0},{16,24},{24,16},{1,9},{9,1},{17,25},{25,17},{2,10},{10... | collective-permute-start | bytes 1572872 | tf_op jit(solution)/shard_map/ppermute | solution.py:10
  21.7 0.8 copy-start.1
  22.5 47.0 %all-gather.29.cloned.1.call-start = ((), (), s32[]{:S(2)}) async-start(), calls=%async_computation.5 | async-start | bytes 2621440 | tf_op jit(solution)/shard_map/all_gather | solution.py:18
  23.3 72.2 %all-gather.33.cloned.1.call-start = ((), (), s32[]{:S(2)}) async-start(), calls=%async_computation.7 | async-start | bytes 1572864 | tf_op jit(solution)/shard_map/all_gather | solution.py:20
  74.1 45.4 %all-gather.19.cloned.1.call-start = ((), (), s32[]{:S(2)}) async-start(), calls=%async_computation | async-start | bytes 2621440 | tf_op jit(solution)/shard_map/all_gather | solution.py:18
  74.7 67.6 %all-gather.31.cloned.1.call-start = ((), (), s32[]{:S(2)}) async-start(), calls=%async_computation.6 | async-start | bytes 1572864 | tf_op jit(solution)/shard_map/all_gather | solution.py:20
  75.2 91.0 %all-gather.21.cloned.1.call-start = ((), (), s32[]{:S(2)}) async-start(), calls=%async_computation.1 | async-start | bytes 2621440 | tf_op jit(solution)/shard_map/all_gather | solution.py:18
  119.5 46.7 %copy-start = (f32[256,512]{1,0:T(8,128)S(1)}, f32[256,512]{1,0:T(8,128)}, u32[]{:S(2)}) copy-start(f32[256,512]{1,0:T(8,128)} %get-tuple-element.9) | copy-start | bytes 1572868
  123.9 65.1 %all-gather.23.cloned.1.call-start = ((), (), s32[]{:S(2)}) async-start(), calls=%async_computation.2 | async-start | bytes 1572864 | tf_op jit(solution)/shard_map/all_gather | solution.py:46
  124.7 46.0 %copy-start.2 = (f32[1,256,1536]{2,1,0:T(8,128)S(1)}, f32[1,256,1536]{2,1,0:T(8,128)}, u32[]{:S(2)}) copy-start(f32[1,256,1536]{2,1,0:T(8,128)} %param.6) | copy-start | bytes 4718596
  124.7 112.3 %all-gather.37.cloned.1.call-start = ((), (), s32[]{:S(2)}) async-start(), calls=%async_computation.9 | async-start | bytes 7864320 | tf_op jit(solution)/shard_map/all_gather | solution.py:43
  125.5 150.1 %all-gather.35.cloned.1.call-start = ((), (), s32[]{:S(2)}) async-start(), calls=%async_computation.8 | async-start | bytes 4718592 | tf_op jit(solution)/shard_map/all_gather | solution.py:53
  170.6 188.5 %all-gather.25.cloned.1.call-start = ((), (), s32[]{:S(2)}) async-start(), calls=%async_computation.3 | async-start | bytes 15728640 | tf_op jit(solution)/shard_map/all_gather | solution.py:52
  170.7 36.6 %collective-permute-start.1 = (f32[256,1536]{1,0:T(8,128)S(1)}, f32[256,1536]{1,0:T(8,128)S(1)}, u32[]{:S(2)}, u32[]{:S(2)}) collective-permute-start(f32[256,1536]{1,0:T(8,128)S(1)} %bitcast.55), channel_id=1, source_target_pairs={{0,8},{8,0},{16,24},{24,16},{1,9},{9,1},{17,25},{25,17},{2,10},{10... | collective-permute-start | bytes 4718600 | tf_op jit(solution)/shard_map/ppermute | solution.py:10
  246.9 158.7 %all-gather.39.cloned.1.call-start = ((), (), s32[]{:S(2)}) async-start(), calls=%async_computation.10 | async-start | bytes 4718592 | tf_op jit(solution)/shard_map/all_gather | solution.py:63
Sparse Core Ops, SparseCore 0:
  22.7 22.6 all-gather.26
  46.9 22.5 all-gather.28
  74.2 21.2 all-gather.32
  96.9 22.5 all-gather.18
  120.9 21.2 all-gather.30
  143.6 22.5 all-gather.20
  167.8 21.2 all-gather.22
  190.6 46.3 all-gather.36
  238.9 36.5 all-gather.34
  276.9 82.0 all-gather.24
  360.6 44.8 all-gather.38
